TPU v7x, 256 devices: a whole 4x4x8 slice. The times are simulated.
256 devices in a mesh: dp: 32 (over x, z), ctx: 8 (over y, core).
Axes of the slice: x: 4, y: 4, z: 8, core: 2. Of those that a mesh axis runs over, the one named last changes fastest.
Arguments:
- hidden: bfloat16 [32, 2048, 4096], P('dp', 'ctx'), may hold values from -6 to 6
- segments: int32 [32, 2048], P('dp', 'ctx'), may hold values from 0 to 15, as said below
- gain: float32 [4096], replicated, may hold values from 0.25 to 1.75
- inv_temp: float32 [], replicated, may hold values from 20 to 50
- positives: int32 [512], P(('dp', 'ctx')), may hold values from 0 to 511, as said below
Outputs:
- grad_hidden: bfloat16 [32, 2048, 4096], P('dp', 'ctx')
- grad_gain: float32 [4096], replicated
- loss: float32 [], replicated
Inputs may be any that keep to these rules, and one draw needn't show every extreme that they name: `segments`: in each sequence the document numbers never fall along positions and every document has one position or more; document 0 covers more than half of the sequence's positions. `positives`: no document is its own positive.
All inputs are finite; a program needn't handle non-finite values.
Results may differ from a plain program's by a relative error of at most 0.0053.
Values may be sent and summed in bfloat16 or wider, within the bound.
A program may use at most 64 MiB of HBM per device.

v0:
```python
import jax
import jax.numpy as jnp
from jax import lax
from jax.sharding import PartitionSpec as P

DOCS_DEV = 2


def normalize_docs(pooled_totals, counts):
    pooled = pooled_totals / counts[:, None]
    rnorm = lax.rsqrt(jnp.sum(pooled * pooled, axis=-1, keepdims=True) + 1e-06)
    return (pooled * rnorm, rnorm)


def body(hidden, segments, gain, inv_temp, positives):
    states = hidden[0].astype(jnp.float32)
    scale_t = lax.rsqrt(jnp.mean(states * states, axis=-1, keepdims=True) + 1e-06)
    normalized_rows = states * scale_t * gain
    ctx_count = lax.axis_size("ctx")
    seq_docs = DOCS_DEV * ctx_count
    document_indicator = (
        segments[0][:, None] == jnp.arange(seq_docs, dtype=jnp.int32)[None, :]
    ).astype(jnp.float32)
    pooled_totals = lax.dot_general(
        document_indicator,
        normalized_rows,
        (((0,), (0,)), ((), ())),
        precision=lax.Precision.HIGHEST,
    )
    counts = jnp.sum(document_indicator, axis=0)
    ctx_rank = lax.axis_index("ctx")
    own_sums, own_counts = (
        lax.psum_scatter(pooled_totals, "ctx", scatter_dimension=0, tiled=True),
        lax.psum_scatter(counts, "ctx", scatter_dimension=0, tiled=True),
    )
    emb_f, rnorm = normalize_docs(own_sums, own_counts)
    emb_own = emb_f.astype(jnp.bfloat16)
    emb_all = lax.all_gather(emb_own, ("dp", "ctx"), axis=0, tiled=True)
    all_docs = emb_all.shape[0]
    row_first = (lax.axis_index("dp") * ctx_count + ctx_rank) * DOCS_DEV
    logits = (
        lax.dot_general(
            emb_own, emb_all, (((1,), (1,)), ((), ())), preferred_element_type=jnp.float32
        )
        * inv_temp
    )
    columns = jnp.arange(all_docs, dtype=jnp.int32)[None, :]
    own_rows = row_first + jnp.arange(DOCS_DEV, dtype=jnp.int32)[:, None]
    pos_mask = (columns == positives[:, None]).astype(jnp.float32)
    logits = jnp.where(columns == own_rows, -1e30, logits)
    top = jnp.max(logits, axis=1, keepdims=True)
    expo = jnp.exp(logits - top)
    total = jnp.sum(expo, axis=1, keepdims=True)
    lse = top[:, 0] + jnp.log(total[:, 0])
    loss_local = jnp.sum(lse - jnp.sum(pos_mask * logits, axis=1)) / all_docs
    gmat = ((expo / total - pos_mask) * (inv_temp / all_docs)).astype(jnp.bfloat16)
    row_grad = jnp.dot(gmat, emb_all, preferred_element_type=jnp.float32)
    grad_rows = lax.all_gather(gmat, ("dp", "ctx"), axis=0, tiled=True)
    grad_cols = lax.dynamic_slice_in_dim(grad_rows, row_first, DOCS_DEV, 1)
    col_grad = lax.dot_general(
        grad_cols, emb_all, (((0,), (0,)), ((), ())), preferred_element_type=jnp.float32
    )
    demb = row_grad + col_grad
    dpool = rnorm * (demb - emb_f * jnp.sum(emb_f * demb, axis=-1, keepdims=True))
    dsum_own = dpool / own_counts[:, None]
    dsum_seq = lax.all_gather(dsum_own, "ctx", axis=0, tiled=True)
    normalized_gradient = jnp.dot(document_indicator, dsum_seq, precision=lax.Precision.HIGHEST)
    gain_local = jnp.sum(normalized_gradient * states * scale_t, axis=0)
    grad_gain, loss = lax.psum((gain_local, loss_local), ("dp", "ctx"))
    grad_out = normalized_gradient * gain
    inner = jnp.mean(grad_out * states, axis=-1, keepdims=True)
    grad_hidden = (scale_t * grad_out - states * scale_t**3 * inner).astype(jnp.bfloat16)
    return (grad_hidden[None], grad_gain, loss)


def solution(mesh):
    return jax.shard_map(
        body,
        mesh=mesh,
        in_specs=(P("dp", "ctx", None), P("dp", "ctx"), P(), P(), P(("dp", "ctx"))),
        out_specs=(P("dp", "ctx", None), P(), P()),
        check_vma=False,
    )
```

profile of v0, /device:TPU:1, one launch (start us, length us, event | category | flops | bytes accessed | tf_op | source)
XLA Modules:
  0.0 389.6 jit_solution(4266364074889755771)
XLA Ops:
  7.2 2.1 fusion
  9.3 4.2 %fusion.2 = f32[16,4096]{1,0:T(8,128)} fusion(bf16[1,256,4096]{2,1,0:T(8,128)(2,1)} %param.5, f32[4096]{0:T(1024)} %param.7, f32[256]{0:T(256)S(1)} %get-tuple-element.12, s32[256]{0:T(256)} %bitcast.26), kind=kOutput, calls=%fused_computation.8 | convolution fusion | flops 204476416 | bytes 2377728 | tf_op jit(solution)/shard_map/dot_general | solution.py:24
  13.6 0.6 dynamic-slice
  14.8 0.1 convert_reduce_fusion
  15.0 15.0 %all-reduce.1 = f32[16]{0:T(128)S(1)} all-reduce(f32[16]{0:T(128)S(1)} %convert_reduce_fusion), channel_id=3, replica_groups=mesh['dp'=32,'ctx'=8] {'ctx'}, use_global_device_ids=true, to_apply=%region_3.0.clone | all-reduce | flops 16 | bytes 128
  30.0 50.8 %all-reduce.5.cloned.1.call-done = f32[16,4096]{1,0:T(8,128)} async-done(((f32[16,4096]{1,0:T(8,128)}), f32[16,4096]{1,0:T(8,128)}) %all-reduce.5.cloned.1.call-update) | async-done | bytes 262160
  80.8 1.1 multiply_reduce_fusion.1
  81.9 0.7 fusion.30
  83.3 119.1 %all-gather.5.cloned.1.call-done = bf16[256,2,4096]{2,1,0:T(2,128)(2,1)} async-done(((bf16[1,2,4096]{2,1,0:T(2,128)(2,1)}), bf16[256,2,4096]{2,1,0:T(2,128)(2,1)}) %all-gather.5.cloned.1.call-update) | async-done | bytes 4194320 | tf_op jit(solution)/shard_map/all_gather | solution.py:38
  202.4 7.2 %reshape.46 = bf16[512,4096]{1,0:T(8,128)(2,1)} reshape(bf16[256,2,4096]{2,1,0:T(2,128)(2,1)} %all-gather.5.cloned.1.call-done) | data formatting | bytes 8388608
  209.6 3.6 fusion.21
  213.3 0.2 select_reduce_fusion
  213.5 0.1 fusion.29
  213.6 0.7 fusion.22
  214.3 0.6 subtract_reduce_fusion
  215.6 67.0 %all-gather.1 = bf16[256,2,512]{2,1,0:T(2,128)(2,1)S(1)} all-gather(bf16[1,2,512]{2,1,0:T(2,128)(2,1)S(1)} %fusion.29), channel_id=1, replica_groups=mesh['dp'=32,'ctx'=8] {'dp','ctx'}, dimensions={0}, use_global_device_ids=true | all-gather | bytes 526336 | tf_op jit(solution)/shard_map/all_gather | solution.py:58
  282.6 0.2 reshape.48
  282.8 3.1 multiply_reduce_fusion
  285.9 0.1 divide_bitcast_fusion
  286.0 12.8 %all-gather.2 = f32[8,2,4096]{2,1,0:T(2,128)S(1)} all-gather(f32[1,2,4096]{2,1,0:T(2,128)S(1)} %divide_bitcast_fusion), channel_id=1, replica_groups=mesh['dp'=32,'ctx'=8] {'ctx'}, dimensions={0}, use_global_device_ids=true | all-gather | bytes 294912 | tf_op jit(solution)/shard_map/all_gather | solution.py:66
  298.8 0.2 reshape.50
  299.0 4.8 %fusion.9 = (f32[4096]{0:T(1024)S(1)}, f32[256]{0:T(256)S(1)}, f32[256,4096]{1,0:T(8,128)}) fusion(bf16[1,256,4096]{2,1,0:T(8,128)(2,1)S(1)} %copy-done.1, f32[256]{0:T(256)S(1)} %get-tuple-element.12, f32[4096]{0:T(1024)S(1)} %copy-done.2, f32[16,4096]{1,0:T(8,128)S(1)} %reshape.50, s32[256]{0:T(256)S(1)} %bitcast.28), kind=kOutput, calls=%fused_computation.14 | convolution fusion | flops 208666368 | bytes 6589440 | tf_op jit(solution)/shard_map/dot_general | solution.py:67
  303.8 74.0 %all-reduce.2 = (f32[4096]{0:T(1024)}, f32[]{:T(128)}) all-reduce(f32[4096]{0:T(1024)S(1)} %get-tuple-element.3, f32[]{:T(128)S(6)} %div.42), channel_id=1, replica_groups=mesh['dp'=32,'ctx'=8] {'dp','ctx'}, use_global_device_ids=true, to_apply=%region_10.11 | all-reduce | flops 4097 | bytes 32776 | tf_op jit(solution)/shard_map/psum | solution.py:69
  377.8 5.0 %fusion.10 = bf16[1,256,4096]{2,1,0:T(8,128)(2,1)} fusion(f32[256,4096]{1,0:T(8,128)} %get-tuple-element.17, bf16[1,256,4096]{2,1,0:T(8,128)(2,1)S(1)} %copy-done.1, f32[256]{0:T(256)S(1)} %broadcast_multiply_fusion, f32[256]{0:T(256)S(1)} %get-tuple-element.11, f32[4096]{0:T(1024)S(1)} %copy-done.2, f32[256]{0:T(256)S(1)} %get-tuple-element.12), kind=kLoop, calls=%fused_computation.15 | loop fusion | flops 7340032 | bytes 8408064 | tf_op jit(solution)/shard_map/broadcast_in_dim | solution.py:73
  (21 shorter events, 0.2 us)
Async XLA Ops:
  7.2 6.4 %copy-start.5 = (u32[256]{0:T(256)S(1)}, u32[256]{0:T(256)}, u32[]{:S(2)}) copy-start(u32[256]{0:T(256)} %constant.40) | copy-start | bytes 3076
  7.2 7.7 %copy-start.4 = (s32[1,256]{1,0:T(1,128)S(1)}, s32[1,256]{1,0:T(1,128)}, u32[]{:S(2)}) copy-start(s32[1,256]{1,0:T(1,128)} %param.6) | copy-start | bytes 3076
  7.2 73.6 %all-reduce.5.cloned.1.call-start = ((), (), s32[]{:S(2)}) async-start(), calls=%async_computation.1 | async-start | bytes 524288
  13.5 188.9 %all-gather.5.cloned.1.call-start = ((), (), s32[]{:S(2)}) async-start(), calls=%async_computation | async-start | bytes 4210688 | tf_op jit(solution)/shard_map/all_gather | solution.py:38
  209.6 3.6 copy-start.3
  209.6 4.0 %copy-start = (bf16[512,4096]{1,0:T(8,128)(2,1)S(1)}, bf16[512,4096]{1,0:T(8,128)(2,1)}, u32[]{:S(2)}) copy-start(bf16[512,4096]{1,0:T(8,128)(2,1)} %reshape.46) | copy-start | bytes 12582916
  214.3 84.7 %copy-start.1 = (bf16[1,256,4096]{2,1,0:T(8,128)(2,1)S(1)}, bf16[1,256,4096]{2,1,0:T(8,128)(2,1)}, u32[]{:S(2)}) copy-start(bf16[1,256,4096]{2,1,0:T(8,128)(2,1)} %param.5) | copy-start | bytes 6291460
  214.3 84.7 %copy-start.2 = (f32[4096]{0:T(1024)S(1)}, f32[4096]{0:T(1024)}, u32[]{:S(2)}) copy-start(f32[4096]{0:T(1024)} %param.7) | copy-start | bytes 49156
Sparse Core Ops, SparseCore 0:
  13.7 67.1 all-reduce.4
  85.1 117.3 all-gather.4
where the time goes:
time: 390 us
  waiting for transfers between devices  170 us (44%)
  blocking collectives  169 us (43%)
  matrix products  16.3 us (4%)
  between operations  16.1 us (4%)
  other arithmetic  10 us (3%)
  local copies, waits for them, and re-layouts  8.27 us (2%)
    all_gather x1, waiting for transfers between devices, body(): emb_all = lax.all_gather(emb_own, ('dp', 'ctx'), axis=0, tiled=True)  119 us
    psum x1, blocking collectives, body(): grad_gain, loss = lax.psum((gain_local, loss_local), ('dp', 'ctx'))  74 us
    all_gather x1, blocking collectives, body(): grad_rows = lax.all_gather(gmat, ('dp', 'ctx'), axis=0, tiled=True)  67 us
    unnamed x3, waiting for transfers between devices  50.8 us
    unnamed x1, blocking collectives  15 us
    all_gather x1, blocking collectives, body(): dsum_seq = lax.all_gather(dsum_own, 'ctx', axis=0, tiled=True)  12.8 us
    unnamed x17, local copies, waits for them, and re-layouts  8.27 us
  transfers between devices with their start and end apart: 2, of which 2 were waited for; matrix products, arithmetic and copies ran while one was open for 0% of the time, Pallas kernels for 0%

commit v1 on v0

--- a/solution.py
+++ b/solution.py
@@ -55,7 +55,8 @@
     loss_local = jnp.sum(lse - jnp.sum(pos_mask * logits, axis=1)) / all_docs
     gmat = ((expo / total - pos_mask) * (inv_temp / all_docs)).astype(jnp.bfloat16)
     row_grad = jnp.dot(gmat, emb_all, preferred_element_type=jnp.float32)
-    grad_rows = lax.all_gather(gmat, ("dp", "ctx"), axis=0, tiled=True)
+    sent = jnp.stack([gmat] * lax.axis_size(("dp", "ctx")))
+    grad_rows = jnp.concatenate(lax.all_to_all(sent, ("dp", "ctx"), 0, 0), axis=0)
     grad_cols = lax.dynamic_slice_in_dim(grad_rows, row_first, DOCS_DEV, 1)
     col_grad = lax.dot_general(
         grad_cols, emb_all, (((0,), (0,)), ((), ())), preferred_element_type=jnp.float32

time: 390 us -> 351 us (0.900)
  blocking collectives: 169 us -> 101 us
  waiting for transfers between devices: 170 us -> 186 us
  starting transfers between devices: 0.08 us -> 8.92 us
    all_gather x1 -> x0, blocking collectives: 67 us -> none  [body(): grad_rows = lax.all_gather(gmat, ('dp', 'ctx'), axis=0, tiled=True)]
    all_to_all x0 -> x1, waiting for transfers between devices: none -> 16.4 us  [body(): lax.all_to_all(sent, ('dp', 'ctx'), 0, 0)]
    all_to_all x0 -> x1, starting transfers between devices: none -> 8.84 us  [body(): lax.all_to_all(sent, ('dp', 'ctx'), 0, 0)]
    unnamed x17 -> x14, local copies, waits for them, and re-layouts: 8.27 us -> 8.07 us
  transfers between devices with their start and end apart: 2 -> 3, of which waited for: 2 -> 3; matrix products, arithmetic and copies ran while one was open for 0% -> 1% of each run, Pallas kernels for 0% -> 0%
where the time goes in v1:
time: 351 us; the launch traced here: 350 us
  waiting for transfers between devices  186 us (53%)
  blocking collectives  101 us (29%)
  matrix products  18.3 us (5%)
  between operations  16.1 us (5%)
  other arithmetic  10 us (3%)
  local copies, waits for them, and re-layouts  9.33 us (3%)
  starting transfers between devices  8.92 us (3%)
    all_gather x1, waiting for transfers between devices, body(): emb_all = lax.all_gather(emb_own, ('dp', 'ctx'), axis=0, tiled=True)  119 us
    psum x1, blocking collectives, body(): grad_gain, loss = lax.psum((gain_local, loss_local), ('dp', 'ctx'))  73.4 us
    unnamed x3, waiting for transfers between devices  50.8 us
    all_to_all x1, waiting for transfers between devices, body(): lax.all_to_all(sent, ('dp', 'ctx'), 0, 0)  16.4 us
    unnamed x1, blocking collectives  15 us
    all_gather x1, blocking collectives, body(): dsum_seq = lax.all_gather(dsum_own, 'ctx', axis=0, tiled=True)  12.6 us
    all_to_all x1, starting transfers between devices, body(): lax.all_to_all(sent, ('dp', 'ctx'), 0, 0)  8.84 us
    unnamed x14, local copies, waits for them, and re-layouts  8.07 us
  transfers between devices with their start and end apart: 3, of which 3 were waited for; matrix products, arithmetic and copies ran while one was open for 1% of the time, Pallas kernels for 0%

profile of v1, /device:TPU:1, one launch (start us, length us, event | category | flops | bytes accessed | tf_op | source)
XLA Modules:
  0.0 350.1 jit_solution(13982006114123147995)
XLA Ops:
  7.2 2.1 fusion
  9.3 4.2 %fusion.2 = f32[16,4096]{1,0:T(8,128)} fusion(bf16[1,256,4096]{2,1,0:T(8,128)(2,1)} %param.5, f32[4096]{0:T(1024)} %param.7, f32[256]{0:T(256)S(1)} %get-tuple-element.12, s32[256]{0:T(256)} %bitcast.24), kind=kOutput, calls=%fused_computation.8 | convolution fusion | flops 204476416 | bytes 2377728 | tf_op jit(solution)/shard_map/dot_general | solution.py:24
  13.6 0.6 dynamic-slice
  14.8 0.1 convert_reduce_fusion
  15.0 15.0 %all-reduce.1 = f32[16]{0:T(128)S(1)} all-reduce(f32[16]{0:T(128)S(1)} %convert_reduce_fusion), channel_id=3, replica_groups=mesh['dp'=32,'ctx'=8] {'ctx'}, use_global_device_ids=true, to_apply=%region_3.0.clone | all-reduce | flops 16 | bytes 128
  30.0 50.8 %all-reduce.5.cloned.1.call-done = f32[16,4096]{1,0:T(8,128)} async-done(((f32[16,4096]{1,0:T(8,128)}), f32[16,4096]{1,0:T(8,128)}) %all-reduce.5.cloned.1.call-update) | async-done | bytes 262160
  80.8 1.1 multiply_reduce_fusion.1
  82.0 0.7 fusion.29
  83.3 119.1 %all-gather.4.cloned.1.call-done = bf16[256,2,4096]{2,1,0:T(2,128)(2,1)} async-done(((bf16[1,2,4096]{2,1,0:T(2,128)(2,1)}), bf16[256,2,4096]{2,1,0:T(2,128)(2,1)}) %all-gather.4.cloned.1.call-update) | async-done | bytes 4194320 | tf_op jit(solution)/shard_map/all_gather | solution.py:38
  202.4 7.2 %reshape.52 = bf16[512,4096]{1,0:T(8,128)(2,1)} reshape(bf16[256,2,4096]{2,1,0:T(2,128)(2,1)} %all-gather.4.cloned.1.call-done) | data formatting | bytes 8388608
  209.6 3.5 fusion.21
  213.2 0.2 select_reduce_fusion
  213.5 1.1 stack.2
  214.5 8.8 %all-to-all-start = ((bf16[256,2,512]{2,1,0:T(2,128)(2,1)}), bf16[256,2,512]{2,1,0:T(2,128)(2,1)S(1)}, u32[]{:S(2)}, u32[]{:S(2)}) async-start(bf16[256,2,512]{2,1,0:T(2,128)(2,1)} %stack.2), calls=%async_computation | async-start | bytes 1048576 | tf_op jit(solution)/shard_map/all_to_all | solution.py:59
  223.4 0.6 subtract_reduce_fusion
  224.6 2.8 fusion.22
  227.5 16.4 %all-to-all-done = bf16[256,2,512]{2,1,0:T(2,128)(2,1)S(1)} async-done(((bf16[256,2,512]{2,1,0:T(2,128)(2,1)}), bf16[256,2,512]{2,1,0:T(2,128)(2,1)S(1)}, u32[]{:S(2)}, u32[]{:S(2)}) %all-to-all-start) | async-done | bytes 524320 | tf_op jit(solution)/shard_map/all_to_all | solution.py:59
  243.9 0.2 reshape.49
  244.1 3.1 multiply_reduce_fusion
  247.3 12.6 %all-gather.1 = f32[8,2,4096]{2,1,0:T(2,128)S(1)} all-gather(f32[1,2,4096]{2,1,0:T(2,128)S(1)} %divide_bitcast_fusion), channel_id=1, replica_groups=mesh['dp'=32,'ctx'=8] {'ctx'}, dimensions={0}, use_global_device_ids=true | all-gather | bytes 294912 | tf_op jit(solution)/shard_map/all_gather | solution.py:67
  259.9 0.2 reshape.54
  260.1 4.8 %fusion.9 = (f32[4096]{0:T(1024)S(1)}, f32[256]{0:T(256)S(1)}, f32[256,4096]{1,0:T(8,128)}) fusion(bf16[1,256,4096]{2,1,0:T(8,128)(2,1)S(1)} %copy-done, f32[256]{0:T(256)S(1)} %get-tuple-element.12, f32[4096]{0:T(1024)S(1)} %copy-done.1, f32[16,4096]{1,0:T(8,128)S(1)} %reshape.54, s32[256]{0:T(256)S(1)} %bitcast.26), kind=kOutput, calls=%fused_computation.14 | convolution fusion | flops 208666368 | bytes 6589440 | tf_op jit(solution)/shard_map/dot_general | solution.py:68
  264.9 73.4 %all-reduce.2 = (f32[4096]{0:T(1024)}, f32[]{:T(128)}) all-reduce(f32[4096]{0:T(1024)S(1)} %get-tuple-element.3, f32[]{:T(128)S(6)} %div.42), channel_id=1, replica_groups=mesh['dp'=32,'ctx'=8] {'dp','ctx'}, use_global_device_ids=true, to_apply=%region_10.11 | all-reduce | flops 4097 | bytes 32776 | tf_op jit(solution)/shard_map/psum | solution.py:70
  338.3 5.0 %fusion.10 = bf16[1,256,4096]{2,1,0:T(8,128)(2,1)} fusion(f32[256,4096]{1,0:T(8,128)} %get-tuple-element.17, bf16[1,256,4096]{2,1,0:T(8,128)(2,1)S(1)} %copy-done, f32[256]{0:T(256)S(1)} %broadcast_multiply_fusion, f32[256]{0:T(256)S(1)} %get-tuple-element.11, f32[4096]{0:T(1024)S(1)} %copy-done.1, f32[256]{0:T(256)S(1)} %get-tuple-element.12), kind=kLoop, calls=%fused_computation.15 | loop fusion | flops 7340032 | bytes 8408064 | tf_op jit(solution)/shard_map/broadcast_in_dim | solution.py:74
  (21 shorter events, 0.4 us)
Async XLA Ops:
  7.2 6.4 %copy-start.4 = (u32[256]{0:T(256)S(1)}, u32[256]{0:T(256)}, u32[]{:S(2)}) copy-start(u32[256]{0:T(256)} %constant.40) | copy-start | bytes 3076
  7.2 7.7 %copy-start.3 = (s32[1,256]{1,0:T(1,128)S(1)}, s32[1,256]{1,0:T(1,128)}, u32[]{:S(2)}) copy-start(s32[1,256]{1,0:T(1,128)} %param.6) | copy-start | bytes 3076
  7.2 73.6 %all-reduce.5.cloned.1.call-start = ((), (), s32[]{:S(2)}) async-start(), calls=%async_computation.2 | async-start | bytes 524288
  13.5 188.9 %all-gather.4.cloned.1.call-start = ((), (), s32[]{:S(2)}) async-start(), calls=%async_computation.1 | async-start | bytes 4210688 | tf_op jit(solution)/shard_map/all_gather | solution.py:38
  209.6 3.5 %copy-start.2 = (s32[2]{0:T(128)S(1)}, s32[2]{0:T(128)}, u32[]{:S(2)}) copy-start(s32[2]{0:T(128)} %param.9) | copy-start | bytes 28
  214.5 29.4 %all-to-all-start = ((bf16[256,2,512]{2,1,0:T(2,128)(2,1)}), bf16[256,2,512]{2,1,0:T(2,128)(2,1)S(1)}, u32[]{:S(2)}, u32[]{:S(2)}) async-start(bf16[256,2,512]{2,1,0:T(2,128)(2,1)} %stack.2), calls=%async_computation | async-start | bytes 1048576 | tf_op jit(solution)/shard_map/all_to_all | solution.py:59
  227.5 32.6 %copy-start = (bf16[1,256,4096]{2,1,0:T(8,128)(2,1)S(1)}, bf16[1,256,4096]{2,1,0:T(8,128)(2,1)}, u32[]{:S(2)}) copy-start(bf16[1,256,4096]{2,1,0:T(8,128)(2,1)} %param.5) | copy-start | bytes 6291460
  227.5 32.6 %copy-start.1 = (f32[4096]{0:T(1024)S(1)}, f32[4096]{0:T(1024)}, u32[]{:S(2)}) copy-start(f32[4096]{0:T(1024)} %param.7) | copy-start | bytes 49156
Sparse Core Ops, SparseCore 0:
  13.7 67.1 all-reduce.4
  85.1 117.3 all-gather.3
